TPU v7x, 32 devices: a whole 2x2x4 slice. The times are simulated.
32 devices in a mesh: phase: 16 (over z, y, x), lat: 2 (over core).
Axes of the slice: x: 2, y: 2, z: 4, core: 2. Of those that a mesh axis runs over, the one named last changes fastest.
Arguments:
- state_now: float32 [3, 64, 1024], P(None, ('lat', 'phase')), may hold values from -4 to 4
- ocean_depth: float32 [64, 1024], P('lat'), may hold values from 0.5 to 1.5
- coriolis: float32 [64], P('lat'), may hold values from -0.4 to 0.4
- phase_times: float32 [16], P('phase'), may hold values from -6 to 6
- phase_weights: float32 [16], P('phase'), may hold values from 0.00625 to 0.25
Outputs:
- state_next: float32 [3, 64, 1024], P(None, ('lat', 'phase'))
- tendency: float32 [3, 64, 1024], P(None, ('lat', 'phase'))
All inputs are finite; a program needn't handle non-finite values.
Results may differ from a plain program's by a relative error of at most 0.00002.
Values sent between devices are 32-bit elements; how exact they have to be, the bound alone decides.
A program may use at most 64 MiB of HBM per device.

v0:
```python
import math

import jax
import jax.numpy as jnp
from jax import lax
from jax.sharding import PartitionSpec as P

DEG = 8
DEPTH = 4


radius_scale = 2.5
time_step = 0.5
series_terms = 20


def extended(shard, sides, width):
    for axis, dim in sides:
        devices, length = (lax.axis_size(axis), shard.shape[dim])
        up = [(i, (i + 1) % devices) for i in range(devices - 1)]
        down = [(j, i) for i, j in up]
        last = lax.slice_in_dim(shard, length - width, length, axis=dim)
        first = lax.slice_in_dim(shard, 0, width, axis=dim)
        before = lax.ppermute(last, axis, up)
        after = lax.ppermute(first, axis, down)
        shard = jnp.concatenate([before, shard, after], axis=dim)
    return shard


def along_lon(values):
    return (jnp.roll(values, -1, axis=-1) - jnp.roll(values, 1, axis=-1)) * 0.5


def along_lat(values):
    return (values[..., 2:, :] - values[..., :-2, :]) * 0.5


def interior(values):
    return values[..., 1:-1, :]


def wave_operator(fields, coefficients):
    height = fields[:, 0]
    eastward = fields[:, 1]
    northward = fields[:, 2]
    depth_field = coefficients[0]
    rotation = coefficients[1]
    out_height = -(along_lon(interior(depth_field * eastward)) + along_lat(depth_field * northward))
    out_east = -along_lon(interior(height)) + interior(rotation * northward)
    out_north = -along_lat(height) - interior(rotation * eastward)
    return jnp.stack([out_height, out_east, out_north], axis=1) / radius_scale


def advection(fields):
    height = fields[:, 0]
    eastward = fields[:, 1]
    northward = fields[:, 2]
    mid_east = interior(eastward)
    mid_north = interior(northward)
    out_height = -(along_lon(interior(height * eastward)) + along_lat(height * northward))
    out_east = -(mid_east * along_lon(mid_east) + mid_north * along_lat(eastward))
    out_north = -(mid_east * along_lon(mid_north) + mid_north * along_lat(northward))
    return jnp.stack([out_height, out_east, out_north], axis=1)


def series_coeffs(sample_time):
    half_time = sample_time * 0.5
    square = half_time * half_time
    result = []
    for degree in range(DEG + 1):
        summed = jnp.zeros_like(sample_time)
        term_sq = jnp.ones_like(sample_time)
        for series in range(series_terms):
            factor = (-1.0) ** series / (math.factorial(series) * math.factorial(series + degree))
            summed = summed + factor * term_sq
            term_sq = term_sq * square
        result.append(summed * half_time**degree)
    return result


def trimmed(values, have, wanted):
    excess = have - wanted
    if excess == 0:
        return values
    return values[:, :, excess : values.shape[2] - excess]


def per_device(state_now, ocean_depth, coriolis, phase_times, phase_weights):
    tile_rows = ocean_depth.shape[0]
    lat_count = lax.axis_size("lat")
    lat_place = lax.axis_index("lat")
    stacked = jnp.stack([ocean_depth, jnp.broadcast_to(coriolis[:, None], ocean_depth.shape)])
    coefficients = extended(stacked, (("lat", 1),), DEPTH)
    global_rows = lat_place * tile_rows - DEPTH + jnp.arange(tile_rows + 2 * DEPTH, dtype=jnp.int32)
    inside = ((global_rows >= 0) & (global_rows < tile_rows * lat_count)).astype(jnp.float32)
    forward = series_coeffs(phase_times)
    backward = series_coeffs(-phase_times)
    sample_count = phase_times.shape[0]

    def band_coeffs(margin):
        return coefficients[:, DEPTH - margin : DEPTH + tile_rows + margin]

    def band_inside(margin):
        return inside[DEPTH - margin : DEPTH + tile_rows + margin][None, None, :, None]

    def exponential(fields, series):
        accumulated = series[0][:, None, None, None] * fields
        previous = None
        current = fields
        width_prev = 0
        width_cur = 0
        for degree in range(1, DEG + 1):
            if (degree - 1) % DEPTH == 0:
                if previous is None:
                    current = extended(current, (("lat", 2),), DEPTH)
                else:
                    joined = jnp.concatenate(
                        [trimmed(previous, width_prev, 0), trimmed(current, width_cur, 0)], axis=0
                    )
                    joined = extended(joined, (("lat", 2),), DEPTH)
                    previous = joined[:sample_count]
                    current = joined[sample_count:]
                    width_prev = DEPTH
                width_cur = DEPTH
            width_new = width_cur - 1
            applied = wave_operator(current, band_coeffs(width_cur))
            if previous is None:
                advanced = applied
            else:
                advanced = 2.0 * applied + trimmed(previous, width_prev, width_new)
            advanced = advanced * band_inside(width_new)
            accumulated = accumulated + 2.0 * series[degree][:, None, None, None] * trimmed(
                advanced, width_new, 0
            )
            previous = current
            width_prev = width_cur
            current = advanced
            width_cur = width_new
        return accumulated

    def averaged(whole_tile):
        samples = whole_tile[None]
        waves = exponential(samples, forward)
        rimmed = extended(waves, (("lat", 2),), 1)
        pulled = advection(rimmed)
        returned = exponential(pulled, backward)
        return jnp.sum(phase_weights[:, None, None, None] * returned, axis=0)

    whole_tile = lax.all_gather(state_now, "phase", axis=1, tiled=True)

    def summed_whole(partial_value):
        return lax.psum(partial_value, "phase")

    first = summed_whole(averaged(whole_tile))
    middle = whole_tile + time_step * first
    second = summed_whole(averaged(middle))
    tendency_tile = 0.5 * (first + second)
    share = state_now.shape[1]
    start = lax.axis_index("phase") * share
    tendency = lax.dynamic_slice_in_dim(tendency_tile, start, share, 1)
    state_next = state_now + time_step * tendency
    return (state_next, tendency)


def solution(mesh):
    placed = (P(None, ("lat", "phase"), None), P("lat", None), P("lat"), P("phase"), P("phase"))
    return jax.shard_map(
        per_device,
        mesh=mesh,
        in_specs=placed,
        out_specs=(P(None, ("lat", "phase"), None), P(None, ("lat", "phase"), None)),
        check_vma=False,
    )
```

profile of v0, /device:TPU:0, one launch (start us, length us, event | category | flops | bytes accessed | tf_op | source)
XLA Modules:
  0.0 368.3 jit_solution(13352655160559666389)
XLA Ops:
  8.0 45.3 %all_gather.3 = f32[3,32,1024]{2,0,1:T(4,128)S(1)} all-gather(f32[3,2,1024]{2,0,1:T(4,128)S(1)} %copy.168), channel_id=1, replica_groups=mesh['phase'=16,'lat'=2] {'phase'}, dimensions={1}, use_global_device_ids=true | all-gather | bytes 417792 | tf_op jit(solution)/shard_map/all_gather | solution.py:149
  53.6 1.4 collective-permute-start.3
  55.0 3.0 collective-permute-start.2
  58.2 1.3 collective-permute-start.1
  59.5 3.0 collective-permute-start
  67.0 1.3 collective-permute-start.5
  68.3 3.0 collective-permute-start.4
  76.5 1.3 collective-permute-start.7
  77.8 3.0 collective-permute-start.6
  82.7 1.3 collective-permute-start.9
  84.0 3.0 collective-permute-start.8
  91.5 1.3 collective-permute-start.11
  92.8 3.2 collective-permute-start.10
  100.2 1.3 fusion.41
  101.6 104.9 %all-reduce.3.cloned.1.call-done = f32[3,32,1024]{2,1,0:T(8,128)} async-done(((f32[3,32,1024]{2,1,0:T(8,128)}), f32[3,32,1024]{2,1,0:T(8,128)}) %all-reduce.3.cloned.1.call-update) | async-done | bytes 393232 | tf_op jit(solution)/shard_map/psum | solution.py:152
  209.1 3.0 collective-permute-start.12
  216.6 1.3 collective-permute-start.15
  217.9 3.0 collective-permute-start.14
  227.0 1.3 collective-permute-start.17
  228.3 3.0 collective-permute-start.16
  234.5 3.3 collective-permute-start.18
  243.2 3.0 collective-permute-start.20
  252.0 107.9 %all-reduce.5.cloned.1.call-done = f32[3,32,1024]{2,1,0:T(8,128)} async-done(((f32[3,32,1024]{2,1,0:T(8,128)}), f32[3,32,1024]{2,1,0:T(8,128)}) %all-reduce.5.cloned.1.call-update) | async-done | bytes 393232 | tf_op jit(solution)/shard_map/psum | solution.py:152
  359.9 1.5 multiply_add_fusion.1
  (380 shorter events, 45.4 us)
Async XLA Ops:
  7.2 199.3 %all-reduce.3.cloned.1.call-start = ((), (), s32[]{:S(2)}) async-start(), calls=%async_computation | async-start | bytes 786432 | tf_op jit(solution)/shard_map/psum | solution.py:152
  53.6 9.8 %collective-permute-start.3 = (f32[1,3,4,1024]{3,2,1,0:T(4,128)S(1)}, f32[1,3,4,1024]{3,2,1,0:T(4,128)S(1)}, u32[]{:S(2)}, u32[]{:S(2)}) collective-permute-start(f32[1,3,4,1024]{3,2,1,0:T(4,128)S(1)} %get-tuple-element.195), channel_id=1, source_target_pairs={{1,0},{3,2},{5,4},{7,6},{9,8},{11,10},{13,12},{15,14},{17,16},{19,... | collective-permute-start | bytes 147464 | tf_op jit(solution)/shard_map/ppermute | solution.py:25
  55.0 8.4 %collective-permute-start.2 = (f32[1,3,4,1024]{3,2,1,0:T(4,128)S(1)}, f32[1,3,4,1024]{3,2,1,0:T(4,128)S(1)}, u32[]{:S(2)}, u32[]{:S(2)}) collective-permute-start(f32[1,3,4,1024]{3,2,1,0:T(4,128)S(1)} %get-tuple-element.194), channel_id=1, source_target_pairs={{0,1},{2,3},{4,5},{6,7},{8,9},{10,11},{12,13},{14,15},{16,17},{18,... | collective-permute-start | bytes 147464 | tf_op jit(solution)/shard_map/ppermute | solution.py:24
  58.2 4.6 %collective-permute-start.1 = (f32[2,4,1024]{2,1,0:T(4,128)S(1)}, f32[2,4,1024]{2,1,0:T(4,128)S(1)}, u32[]{:S(2)}, u32[]{:S(2)}) collective-permute-start(f32[2,4,1024]{2,1,0:T(4,128)S(1)} %get-tuple-element.205), channel_id=1, source_target_pairs={{1,0},{3,2},{5,4},{7,6},{9,8},{11,10},{13,12},{15,14},{17,16},{19,... | collective-permute-start | bytes 98312 | tf_op jit(solution)/shard_map/ppermute | solution.py:25
  59.5 3.9 %collective-permute-start = (f32[2,4,1024]{2,1,0:T(4,128)S(1)}, f32[2,4,1024]{2,1,0:T(4,128)S(1)}, u32[]{:S(2)}, u32[]{:S(2)}) collective-permute-start(f32[2,4,1024]{2,1,0:T(4,128)S(1)} %get-tuple-element.204), channel_id=1, source_target_pairs={{0,1},{2,3},{4,5},{6,7},{8,9},{10,11},{12,13},{14,15},{16,17},{18,... | collective-permute-start | bytes 98312 | tf_op jit(solution)/shard_map/ppermute | solution.py:24
  67.0 5.3 %collective-permute-start.5 = (f32[2,3,4,1024]{3,2,1,0:T(4,128)S(1)}, f32[2,3,4,1024]{3,2,1,0:T(4,128)S(1)}, u32[]{:S(2)}, u32[]{:S(2)}) collective-permute-start(f32[2,3,4,1024]{3,2,1,0:T(4,128)S(1)} %get-tuple-element.91), channel_id=1, source_target_pairs={{1,0},{3,2},{5,4},{7,6},{9,8},{11,10},{13,12},{15,14},{17,16},{19,... | collective-permute-start | bytes 294920 | tf_op jit(solution)/shard_map/ppermute | solution.py:25
  68.3 4.0 %collective-permute-start.4 = (f32[2,3,4,1024]{3,2,1,0:T(4,128)S(1)}, f32[2,3,4,1024]{3,2,1,0:T(4,128)S(1)}, u32[]{:S(2)}, u32[]{:S(2)}) collective-permute-start(f32[2,3,4,1024]{3,2,1,0:T(4,128)S(1)} %get-tuple-element.90), channel_id=1, source_target_pairs={{0,1},{2,3},{4,5},{6,7},{8,9},{10,11},{12,13},{14,15},{16,17},{18,... | collective-permute-start | bytes 294920 | tf_op jit(solution)/shard_map/ppermute | solution.py:24
  76.5 4.3 %collective-permute-start.7 = (f32[1,3,1,1024]{3,2,1,0:T(1,128)S(1)}, f32[1,3,1,1024]{3,2,1,0:T(1,128)S(1)}, u32[]{:S(2)}, u32[]{:S(2)}) collective-permute-start(f32[1,3,1,1024]{3,2,1,0:T(1,128)S(1)} %get-tuple-element.193), channel_id=1, source_target_pairs={{1,0},{3,2},{5,4},{7,6},{9,8},{11,10},{13,12},{15,14},{17,16},{19,... | collective-permute-start | bytes 36872 | tf_op jit(solution)/shard_map/ppermute | solution.py:25
  77.8 3.9 %collective-permute-start.6 = (f32[1,3,1,1024]{3,2,1,0:T(1,128)S(1)}, f32[1,3,1,1024]{3,2,1,0:T(1,128)S(1)}, u32[]{:S(2)}, u32[]{:S(2)}) collective-permute-start(f32[1,3,1,1024]{3,2,1,0:T(1,128)S(1)} %get-tuple-element.192), channel_id=1, source_target_pairs={{0,1},{2,3},{4,5},{6,7},{8,9},{10,11},{12,13},{14,15},{16,17},{18,... | collective-permute-start | bytes 36872 | tf_op jit(solution)/shard_map/ppermute | solution.py:24
  82.7 4.3 %collective-permute-start.9 = (f32[1,3,4,1024]{3,2,1,0:T(4,128)S(1)}, f32[1,3,4,1024]{3,2,1,0:T(4,128)S(1)}, u32[]{:S(2)}, u32[]{:S(2)}) collective-permute-start(f32[1,3,4,1024]{3,2,1,0:T(4,128)S(1)} %get-tuple-element.191), channel_id=1, source_target_pairs={{1,0},{3,2},{5,4},{7,6},{9,8},{11,10},{13,12},{15,14},{17,16},{19,... | collective-permute-start | bytes 147464 | tf_op jit(solution)/shard_map/ppermute | solution.py:25
  84.0 3.9 %collective-permute-start.8 = (f32[1,3,4,1024]{3,2,1,0:T(4,128)S(1)}, f32[1,3,4,1024]{3,2,1,0:T(4,128)S(1)}, u32[]{:S(2)}, u32[]{:S(2)}) collective-permute-start(f32[1,3,4,1024]{3,2,1,0:T(4,128)S(1)} %get-tuple-element.190), channel_id=1, source_target_pairs={{0,1},{2,3},{4,5},{6,7},{8,9},{10,11},{12,13},{14,15},{16,17},{18,... | collective-permute-start | bytes 147464 | tf_op jit(solution)/shard_map/ppermute | solution.py:24
  91.5 5.2 %collective-permute-start.11 = (f32[2,3,4,1024]{3,2,1,0:T(4,128)S(1)}, f32[2,3,4,1024]{3,2,1,0:T(4,128)S(1)}, u32[]{:S(2)}, u32[]{:S(2)}) collective-permute-start(f32[2,3,4,1024]{3,2,1,0:T(4,128)S(1)} %get-tuple-element.89), channel_id=1, source_target_pairs={{1,0},{3,2},{5,4},{7,6},{9,8},{11,10},{13,12},{15,14},{17,16},{19,... | collective-permute-start | bytes 294920 | tf_op jit(solution)/shard_map/ppermute | solution.py:25
  92.8 4.0 %collective-permute-start.10 = (f32[2,3,4,1024]{3,2,1,0:T(4,128)S(1)}, f32[2,3,4,1024]{3,2,1,0:T(4,128)S(1)}, u32[]{:S(2)}, u32[]{:S(2)}) collective-permute-start(f32[2,3,4,1024]{3,2,1,0:T(4,128)S(1)} %get-tuple-element.88), channel_id=1, source_target_pairs={{0,1},{2,3},{4,5},{6,7},{8,9},{10,11},{12,13},{14,15},{16,17},{18,... | collective-permute-start | bytes 294920 | tf_op jit(solution)/shard_map/ppermute | solution.py:24
  101.6 258.3 %all-reduce.5.cloned.1.call-start = ((), (), s32[]{:S(2)}) async-start(), calls=%async_computation.1 | async-start | bytes 786432 | tf_op jit(solution)/shard_map/psum | solution.py:152
  207.8 4.3 %collective-permute-start.13 = (f32[1,3,4,1024]{3,2,1,0:T(4,128)S(1)}, f32[1,3,4,1024]{3,2,1,0:T(4,128)S(1)}, u32[]{:S(2)}, u32[]{:S(2)}) collective-permute-start(f32[1,3,4,1024]{3,2,1,0:T(4,128)S(1)} %get-tuple-element.189), channel_id=1, source_target_pairs={{1,0},{3,2},{5,4},{7,6},{9,8},{11,10},{13,12},{15,14},{17,16},{19,... | collective-permute-start | bytes 147464 | tf_op jit(solution)/shard_map/ppermute | solution.py:25
  209.1 3.9 %collective-permute-start.12 = (f32[1,3,4,1024]{3,2,1,0:T(4,128)S(1)}, f32[1,3,4,1024]{3,2,1,0:T(4,128)S(1)}, u32[]{:S(2)}, u32[]{:S(2)}) collective-permute-start(f32[1,3,4,1024]{3,2,1,0:T(4,128)S(1)} %get-tuple-element.188), channel_id=1, source_target_pairs={{0,1},{2,3},{4,5},{6,7},{8,9},{10,11},{12,13},{14,15},{16,17},{18,... | collective-permute-start | bytes 147464 | tf_op jit(solution)/shard_map/ppermute | solution.py:24
  216.6 4.3 %collective-permute-start.15 = (f32[2,3,4,1024]{3,2,1,0:T(4,128)S(1)}, f32[2,3,4,1024]{3,2,1,0:T(4,128)S(1)}, u32[]{:S(2)}, u32[]{:S(2)}) collective-permute-start(f32[2,3,4,1024]{3,2,1,0:T(4,128)S(1)} %get-tuple-element.87), channel_id=1, source_target_pairs={{1,0},{3,2},{5,4},{7,6},{9,8},{11,10},{13,12},{15,14},{17,16},{19,... | collective-permute-start | bytes 294920 | tf_op jit(solution)/shard_map/ppermute | solution.py:25
  217.9 4.0 %collective-permute-start.14 = (f32[2,3,4,1024]{3,2,1,0:T(4,128)S(1)}, f32[2,3,4,1024]{3,2,1,0:T(4,128)S(1)}, u32[]{:S(2)}, u32[]{:S(2)}) collective-permute-start(f32[2,3,4,1024]{3,2,1,0:T(4,128)S(1)} %get-tuple-element.86), channel_id=1, source_target_pairs={{0,1},{2,3},{4,5},{6,7},{8,9},{10,11},{12,13},{14,15},{16,17},{18,... | collective-permute-start | bytes 294920 | tf_op jit(solution)/shard_map/ppermute | solution.py:24
  227.0 4.3 %collective-permute-start.17 = (f32[1,3,1,1024]{3,2,1,0:T(1,128)S(1)}, f32[1,3,1,1024]{3,2,1,0:T(1,128)S(1)}, u32[]{:S(2)}, u32[]{:S(2)}) collective-permute-start(f32[1,3,1,1024]{3,2,1,0:T(1,128)S(1)} %get-tuple-element.187), channel_id=1, source_target_pairs={{1,0},{3,2},{5,4},{7,6},{9,8},{11,10},{13,12},{15,14},{17,16},{19,... | collective-permute-start | bytes 36872 | tf_op jit(solution)/shard_map/ppermute | solution.py:25
  228.3 3.9 %collective-permute-start.16 = (f32[1,3,1,1024]{3,2,1,0:T(1,128)S(1)}, f32[1,3,1,1024]{3,2,1,0:T(1,128)S(1)}, u32[]{:S(2)}, u32[]{:S(2)}) collective-permute-start(f32[1,3,1,1024]{3,2,1,0:T(1,128)S(1)} %get-tuple-element.186), channel_id=1, source_target_pairs={{0,1},{2,3},{4,5},{6,7},{8,9},{10,11},{12,13},{14,15},{16,17},{18,... | collective-permute-start | bytes 36872 | tf_op jit(solution)/shard_map/ppermute | solution.py:24
  233.2 4.6 %collective-permute-start.19 = (f32[1,3,4,1024]{3,2,1,0:T(4,128)S(1)}, f32[1,3,4,1024]{3,2,1,0:T(4,128)S(1)}, u32[]{:S(2)}, u32[]{:S(2)}) collective-permute-start(f32[1,3,4,1024]{3,2,1,0:T(4,128)S(1)} %get-tuple-element.185), channel_id=1, source_target_pairs={{1,0},{3,2},{5,4},{7,6},{9,8},{11,10},{13,12},{15,14},{17,16},{19,... | collective-permute-start | bytes 147464 | tf_op jit(solution)/shard_map/ppermute | solution.py:25
  234.5 3.9 %collective-permute-start.18 = (f32[1,3,4,1024]{3,2,1,0:T(4,128)S(1)}, f32[1,3,4,1024]{3,2,1,0:T(4,128)S(1)}, u32[]{:S(2)}, u32[]{:S(2)}) collective-permute-start(f32[1,3,4,1024]{3,2,1,0:T(4,128)S(1)} %get-tuple-element.184), channel_id=1, source_target_pairs={{0,1},{2,3},{4,5},{6,7},{8,9},{10,11},{12,13},{14,15},{16,17},{18,... | collective-permute-start | bytes 147464 | tf_op jit(solution)/shard_map/ppermute | solution.py:24
  241.9 4.3 %collective-permute-start.21 = (f32[2,3,4,1024]{3,2,1,0:T(4,128)S(1)}, f32[2,3,4,1024]{3,2,1,0:T(4,128)S(1)}, u32[]{:S(2)}, u32[]{:S(2)}) collective-permute-start(f32[2,3,4,1024]{3,2,1,0:T(4,128)S(1)} %get-tuple-element.85), channel_id=1, source_target_pairs={{1,0},{3,2},{5,4},{7,6},{9,8},{11,10},{13,12},{15,14},{17,16},{19,... | collective-permute-start | bytes 294920 | tf_op jit(solution)/shard_map/ppermute | solution.py:25
  243.2 4.0 %collective-permute-start.20 = (f32[2,3,4,1024]{3,2,1,0:T(4,128)S(1)}, f32[2,3,4,1024]{3,2,1,0:T(4,128)S(1)}, u32[]{:S(2)}, u32[]{:S(2)}) collective-permute-start(f32[2,3,4,1024]{3,2,1,0:T(4,128)S(1)} %get-tuple-element.84), channel_id=1, source_target_pairs={{0,1},{2,3},{4,5},{6,7},{8,9},{10,11},{12,13},{14,15},{16,17},{18,... | collective-permute-start | bytes 294920 | tf_op jit(solution)/shard_map/ppermute | solution.py:24
  (4 other events, 118.0 us)
Sparse Core Ops, SparseCore 0:
  101.7 104.7 all-reduce.2
  252.1 107.7 all-reduce.4
where the time goes:
time: 369 us; the launch traced here: 368 us
  waiting for transfers between devices  219 us (59%)
  starting transfers between devices  48.2 us (13%)
  blocking collectives  45.3 us (12%)
  other arithmetic  21.8 us (6%)
  between operations  17.7 us (5%)
  local copies, waits for them, and re-layouts  16.1 us (4%)
    psum x2, waiting for transfers between devices, summed_whole(): return lax.psum(partial_value, 'phase')  213 us
    all_gather x1, blocking collectives, per_device(): whole_tile = lax.all_gather(state_now, 'phase', axis=1, tiled=True)  45.3 us
    ppermute x11, starting transfers between devices, extended(): before = lax.ppermute(last, axis, up)  33.8 us
    ppermute x11, starting transfers between devices, extended(): after = lax.ppermute(first, axis, down)  14.3 us
    slice x140, local copies, waits for them, and re-layouts, along_lon(): return (jnp.roll(values, -1, axis=-1) - jnp.roll(values, 1, axis=-1)) * 0.5  12.7 us
    another operation x63, other arithmetic, wave_operator(): return jnp.stack([out_height, out_east, out_north], axis=1) / radius_scale  7.91 us
  transfers between devices with their start and end apart: 24, of which 10 were waited for; matrix products, arithmetic and copies ran while one was open for 0% of the time, Pallas kernels for 0%

commit v1 on v0

v1 whole, which is shorter than its diff:
```python
import functools
import math

import jax
import jax.numpy as jnp
from jax import lax
from jax.experimental import pallas as pl
from jax.experimental.pallas import tpu as pltpu
from jax.sharding import PartitionSpec as P

DEG = 8
HALO = 2 * DEG + 1
BLOCK = 8
LANES = 128
SUBLANES = 8

radius_scale = 2.5
time_step = 0.5
series_terms = 20

HEIGHT_SCALE = 1.0 / radius_scale
DEPTH_SCALE = 1.0 / (radius_scale * radius_scale)
ROTATION_SCALE = 2.0 / radius_scale


def kernel(
    phases,
    lats,
    state,
    depth,
    coriolis,
    times,
    weights,
    next_out,
    tend_out,
    own,
    gathered,
    window,
    coef_field,
    even,
    odd,
    waves,
    pulled,
    partial,
    parts,
    first,
    series,
    gather_send,
    gather_recv,
    sum_send,
    sum_recv,
    halo_send,
    halo_recv,
):
    rows, share = depth.shape[0], state.shape[1]
    me, lat = lax.axis_index("phase"), lax.axis_index("lat")
    below = (lat + lats - 1) // lats
    above = (2 * lats - 2 - lat) // lats
    span = window.shape[2]

    zero = jnp.zeros((HALO, SUBLANES, LANES), jnp.float32)
    for array in (window.at[0], window.at[1]):
        for field in range(3):
            array[field, 0:HALO] = zero
            array[field, HALO + rows : span] = zero
    for field in range(2):
        coef_field[field, 0:HALO] = zero
        coef_field[field, HALO + rows : span] = zero

    barrier = pltpu.get_barrier_semaphore()

    def greet(step, carry):
        peer = lax.rem(me + step, phases)
        pl.semaphore_signal(barrier, inc=1, device_id={"phase": peer})
        return carry

    lax.fori_loop(1, phases, greet, 0)

    @pl.when(lat > 0)
    def _():
        pl.semaphore_signal(barrier, inc=1, device_id={"lat": lat - 1})

    @pl.when(lat < lats - 1)
    def _():
        pl.semaphore_signal(barrier, inc=1, device_id={"lat": lat + 1})

    for s in range(SUBLANES):
        lanes = pl.ds(s * LANES, LANES)
        for field in range(3):
            piece = state[field, :, lanes]
            own[field, :, s, :] = piece * HEIGHT_SCALE if field == 0 else piece
        coef_field[0, HALO : HALO + rows, s, :] = depth[:, lanes] * DEPTH_SCALE
    for row in range(rows):
        coef_field[1, HALO + row] = jnp.full((SUBLANES, LANES), coriolis[row] * ROTATION_SCALE, jnp.float32)
    gathered[0, :, pl.ds(me * share, share)] = own[...]

    half_time = jnp.full((SUBLANES, LANES), times[0] * 0.5, jnp.float32)
    weight = jnp.full((SUBLANES, LANES), weights[0], jnp.float32)
    square = half_time * half_time
    power = jnp.ones_like(half_time)
    for degree in range(DEG + 1):
        summed = jnp.zeros_like(square)
        for term in reversed(range(series_terms)):
            factor = (-1.0) ** term / (math.factorial(term) * math.factorial(term + degree))
            summed = summed * square + factor
        value = summed * power
        if degree > 0:
            value = 2.0 * value
        series[0, degree] = value
        series[1, degree] = weight * (value if degree % 2 == 0 else -value)
        power = power * half_time

    zero = jnp.zeros((span, SUBLANES, LANES), jnp.float32)
    for field in range(3):
        waves[field] = zero
        pulled[field] = zero

    pl.semaphore_wait(barrier, phases - 1 + below + above)

    def gather_copy(which, step, sending):
        peer = lax.rem(me + step, phases)
        at = pl.ds(me * share, share)
        return pltpu.make_async_remote_copy(
            src_ref=gathered.at[which, :, at],
            dst_ref=gathered.at[which, :, at],
            send_sem=gather_send.at[which, step],
            recv_sem=gather_recv.at[which, step],
            device_id={"phase": peer},
        )

    def sum_copy(which, step):
        peer = lax.rem(me + step, phases)
        return pltpu.make_async_remote_copy(
            src_ref=partial.at[which, :, pl.ds(peer * share, share)],
            dst_ref=parts.at[which, step],
            send_sem=sum_send.at[which, step],
            recv_sem=sum_recv.at[which, step],
            device_id={"phase": peer},
        )

    def each_peer(fn):
        def body(step, carry):
            fn(step)
            return carry

        lax.fori_loop(1, phases, body, 0)

    def edge_copies(array, index):
        up = pltpu.make_async_remote_copy(
            src_ref=array.at[:, pl.ds(rows, HALO)],
            dst_ref=array.at[:, pl.ds(0, HALO)],
            send_sem=halo_send.at[index, 0],
            recv_sem=halo_recv.at[index, 0],
            device_id={"lat": lat + 1},
        )
        down = pltpu.make_async_remote_copy(
            src_ref=array.at[:, pl.ds(HALO, HALO)],
            dst_ref=array.at[:, pl.ds(HALO + rows, HALO)],
            send_sem=halo_send.at[index, 1],
            recv_sem=halo_recv.at[index, 1],
            device_id={"lat": lat - 1},
        )
        return up, down

    def edges_start(array, index):
        up, down = edge_copies(array, index)
        pl.when(lat < lats - 1)(up.start)
        pl.when(lat > 0)(down.start)

    def edges_wait(array, index):
        up, down = edge_copies(array, index)

        @pl.when(lat < lats - 1)
        def _():
            up.wait_send()
            down.wait_recv()

        @pl.when(lat > 0)
        def _():
            down.wait_send()
            up.wait_recv()

    lane = lax.broadcasted_iota(jnp.int32, (BLOCK, SUBLANES, LANES), 2)
    last_lane, first_lane = lane == LANES - 1, lane == 0

    def lon_diff(values):
        after = pltpu.roll(values, LANES - 1, 2)
        after = jnp.where(last_lane, pltpu.roll(after, SUBLANES - 1, 1), after)
        before = pltpu.roll(values, 1, 2)
        before = jnp.where(first_lane, pltpu.roll(before, 1, 1), before)
        return after - before

    def for_blocks(margin, fn):
        start = HALO - margin * below

        def body(i, carry):
            fn(start + i * BLOCK)
            return carry

        if lats == 2:
            lax.fori_loop(0, (rows + margin) // BLOCK, body, 0, unroll=True)
        else:
            lax.fori_loop(0, (rows + margin * (below + above)) // BLOCK, body, 0)

    def twice_operator(source, at):
        mid, wide = pl.ds(at, BLOCK), pl.ds(at - 1, BLOCK + 2)
        height = source[0, wide]
        east = source[1, mid]
        north = source[2, wide]
        flux = coef_field[0, wide] * north
        rotation = coef_field[1, mid]
        height_part = lon_diff(coef_field[0, mid] * east) + (flux[2:] - flux[:-2])
        east_part = lon_diff(height[1:-1]) - rotation * north[1:-1]
        north_part = (height[2:] - height[:-2]) + rotation * east
        return height_part, east_part, north_part

    def clenshaw(target, source, base, factor, margin):
        def body(at):
            mid = pl.ds(at, BLOCK)
            applied = twice_operator(source, at)
            for field in range(3):
                target[field, mid] = (factor * base[field, mid] + target[field, mid]) - applied[field]

        for_blocks(margin, body)

    def exponential(base, direction, margin, store, last_margin):
        top = series[direction, DEG]
        for field in range(3):
            even[field] = top * base[field]
            odd[field] = jnp.zeros((span, SUBLANES, LANES), jnp.float32)

        def two_steps(j, carry):
            clenshaw(odd, even, base, series[direction, DEG - 1 - 2 * j], margin)
            clenshaw(even, odd, base, series[direction, DEG - 2 - 2 * j], margin)
            return carry

        lax.fori_loop(0, DEG // 2 - 1, two_steps, 0)
        clenshaw(odd, even, base, series[direction, 1], margin)
        factor = series[direction, 0]

        def body(at):
            mid = pl.ds(at, BLOCK)
            applied = twice_operator(odd, at)
            for field in range(3):
                store(field, at, (factor * base[field, mid] + even[field, mid]) - 0.5 * applied[field])

        for_blocks(last_margin, body)

    def advect(at):
        mid, wide = pl.ds(at, BLOCK), pl.ds(at - 1, BLOCK + 2)
        height, east, north = waves[0, wide], waves[1, wide], waves[2, wide]
        flux = height * north
        mid_east, mid_north = 0.5 * east[1:-1], 0.5 * north[1:-1]
        pulled[0, mid] = -0.5 * (lon_diff(height[1:-1] * east[1:-1]) + (flux[2:] - flux[:-2]))
        pulled[1, mid] = -(mid_east * lon_diff(east[1:-1]) + mid_north * (east[2:] - east[:-2]))
        pulled[2, mid] = -(mid_east * lon_diff(north[1:-1]) + mid_north * (north[2:] - north[:-2]))

    edges_start(coef_field, 2)
    each_peer(lambda step: gather_copy(0, step, True).start())

    for which in range(2):
        each_peer(lambda step: gather_copy(which, step, False).wait())
        tile = window.at[which]
        for field in range(3):
            tile[field, HALO : HALO + rows] = gathered[which, field]
        edges_start(tile, which)
        if which == 0:
            edges_wait(coef_field, 2)
        edges_wait(tile, which)

        def keep_wave(field, at, value):
            waves[field, pl.ds(at, BLOCK)] = value

        def keep_partial(field, at, value):
            partial[which, field, pl.ds(at - HALO, BLOCK)] = value

        exponential(tile, 0, 2 * DEG, keep_wave, 2 * DEG)
        for_blocks(DEG, advect)
        exponential(pulled, 1, DEG, keep_partial, 0)

        each_peer(lambda step: sum_copy(which, step).start())
        total = partial[which, :, pl.ds(me * share, share)]
        each_peer(lambda step: sum_copy(which, step).wait())
        for step in range(1, phases):
            total = total + parts[which, step]
        if which == 0:
            first[...] = total
            gathered[1, :, pl.ds(me * share, share)] = own[...] + time_step * total
            each_peer(lambda step: gather_copy(1, step, True).start())
        else:
            first[...] = 0.5 * (first[...] + total)

    for s in range(SUBLANES):
        lanes = pl.ds(s * LANES, LANES)
        for field in range(3):
            piece = first[field, :, s, :]
            if field == 0:
                piece = piece * radius_scale
            tend_out[field, :, lanes] = piece
            next_out[field, :, lanes] = state[field, :, lanes] + time_step * piece


def per_device(phases, lats, state_now, ocean_depth, coriolis, phase_times, phase_weights):
    rows, share = ocean_depth.shape[0], state_now.shape[1]
    span = rows + 2 * HALO
    tile = (SUBLANES, LANES)
    vmem = pl.BlockSpec(memory_space=pltpu.VMEM)
    smem = pl.BlockSpec(memory_space=pltpu.SMEM)
    out = jax.ShapeDtypeStruct(state_now.shape, jnp.float32)

    def scratch(*shape):
        return pltpu.VMEM(shape + tile, jnp.float32)

    return pl.pallas_call(
        functools.partial(kernel, phases, lats),
        out_shape=(out, out),
        in_specs=[vmem, vmem, smem, smem, smem],
        out_specs=(vmem, vmem),
        scratch_shapes=[
            scratch(3, share),
            scratch(2, 3, rows),
            scratch(2, 3, span),
            scratch(2, span),
            scratch(3, span),
            scratch(3, span),
            scratch(3, span),
            scratch(3, span),
            scratch(2, 3, rows),
            scratch(2, phases, 3, share),
            scratch(3, share),
            scratch(2, DEG + 1),
            pltpu.SemaphoreType.DMA((2, phases)),
            pltpu.SemaphoreType.DMA((2, phases)),
            pltpu.SemaphoreType.DMA((2, phases)),
            pltpu.SemaphoreType.DMA((2, phases)),
            pltpu.SemaphoreType.DMA((3, 2)),
            pltpu.SemaphoreType.DMA((3, 2)),
        ],
        compiler_params=pltpu.CompilerParams(collective_id=0, has_side_effects=True),
    )(state_now, ocean_depth, coriolis, phase_times, phase_weights)


def solution(mesh):
    placed = (P(None, ("lat", "phase"), None), P("lat", None), P("lat"), P("phase"), P("phase"))
    return jax.shard_map(
        functools.partial(per_device, mesh.shape["phase"], mesh.shape["lat"]),
        mesh=mesh,
        in_specs=placed,
        out_specs=(P(None, ("lat", "phase"), None), P(None, ("lat", "phase"), None)),
        check_vma=False,
    )
```

time: 369 us -> 65.2 us (0.18)
  waiting for transfers between devices: 219 us -> 0 us
  Pallas kernels: 0 us -> 60.3 us
  starting transfers between devices: 48.2 us -> 0 us
  blocking collectives: 45.3 us -> 0 us
  other arithmetic: 21.8 us -> 0 us
  between operations: 17.7 us -> 1.94 us
  local copies, waits for them, and re-layouts: 16.1 us -> 1.96 us
    psum x2 -> x0, waiting for transfers between devices: 213 us -> none  [summed_whole(): return lax.psum(partial_value, 'phase')]
    pallas_call x0 -> x1, Pallas kernels: none -> 60.3 us  [per_device(): pl.pallas_call(functools.partial(kernel, phases, lats), out_shape=(out, o...]
    ppermute x22 -> x0, starting transfers between devices: 48.1 us -> none  [the longest x11 33.8 us: extended(): before = lax.ppermute(last, axis, up)]
    all_gather x1 -> x0, blocking collectives: 45.3 us -> none  [per_device(): whole_tile = lax.all_gather(state_now, 'phase', axis=1, tiled=True)]
    slice x153 -> x0, local copies, waits for them, and re-layouts: 13.2 us -> none  [the longest x140 12.7 us: along_lon(): return (jnp.roll(values, -1, axis=-1) - jnp.roll(values, 1, axis=-1)) * 0.5]
    another operation x69 -> x0, other arithmetic: 8.5 us -> none  [the longest x63 7.91 us: wave_operator(): return jnp.stack([out_height, out_east, out_north], axis=1) / radius_scale]
    ppermute x22 -> x0, waiting for transfers between devices: 6.37 us -> none  [the longest x11 6.34 us: extended(): before = lax.ppermute(last, axis, up)]
    mul x62 -> x0, other arithmetic: 5.03 us -> none  [the longest x28 3.61 us: exponential(): advanced = advanced * band_inside(width_new)]
  transfers between devices with their start and end apart: 24 -> 0, of which waited for: 10 -> 0; matrix products, arithmetic and copies ran while one was open for 0% -> 0% of each run, Pallas kernels for 0% -> 0%
where the time goes in v1:
time: 65.2 us; the launch traced here: 64.2 us
  Pallas kernels  60.3 us (92%)
  local copies, waits for them, and re-layouts  1.96 us (3%)
  between operations  1.94 us (3%)
    pallas_call x1, Pallas kernels, per_device(): pl.pallas_call(functools.partial(kernel, phases, lats), out_shape=(out, o...  60.3 us
    unnamed x4, local copies, waits for them, and re-layouts  1.96 us

profile of v1, /device:TPU:0, one launch (start us, length us, event | category | flops | bytes accessed | tf_op | source)
XLA Modules:
  0.0 64.2 jit_solution(11780381950379502640)
XLA Ops:
  1.9 60.3 %shard_map.68 = (f32[3,2,1024]{2,1,0:T(2,128)}, f32[3,2,1024]{2,1,0:T(2,128)}) custom-call(f32[3,2,1024]{2,1,0:T(2,128)} %state.1, f32[32,1024]{1,0:T(8,128)} %depth.1, f32[32]{0:T(128)} %coriolis.1, f32[1]{0:T(128)S(6)} %copy.9.times, f32[1]{0:T(128)S(6)} %copy.10.weights), custom_call_target="tpu_custom_call" | custom-call | tf_op jit(solution)/shard_map/pallas_call | solution.py:314
  62.3 0.0 copy-start
  62.3 1.4 %copy.11 = f32[3,2,1024]{2,1,0:T(2,128)} copy(f32[3,2,1024]{2,1,0:T(2,128)} %get-tuple-element.4) | data formatting | bytes 49152
  63.6 0.0 copy-done
  63.6 0.6 copy.12
Async XLA Ops:
  62.3 1.4 %copy-start = (f32[3,2,1024]{2,1,0:T(2,128)S(1)}, f32[3,2,1024]{2,1,0:T(2,128)}, u32[]{:S(2)}) copy-start(f32[3,2,1024]{2,1,0:T(2,128)} %get-tuple-element.5) | copy-start | bytes 73732

commit v2 on v1

--- a/solution.py
+++ b/solution.py
@@ -21,6 +21,22 @@
 HEIGHT_SCALE = 1.0 / radius_scale
 DEPTH_SCALE = 1.0 / (radius_scale * radius_scale)
 ROTATION_SCALE = 2.0 / radius_scale
+
+
+def slabs_of(phases):
+    return 4 if phases % 4 == 0 else 1
+
+
+def partner(index, step, count):
+    if count == 4:
+        return [index, index + 1 - 2 * lax.rem(index, 2), lax.rem(index + 2, 4), 3 - index][step]
+    return lax.rem(index + step, count)
+
+
+def source_of(index, step, count):
+    if count == 4:
+        return partner(index, step, count)
+    return lax.rem(index + count - step, count)
 
 
 def kernel(
@@ -43,17 +59,21 @@
     pulled,
     partial,
     parts,
+    staged,
     first,
     series,
-    gather_send,
-    gather_recv,
-    sum_send,
-    sum_recv,
+    outer_send,
+    outer_recv,
+    inner_send,
+    inner_recv,
     halo_send,
     halo_recv,
 ):
     rows, share = depth.shape[0], state.shape[1]
     me, lat = lax.axis_index("phase"), lax.axis_index("lat")
+    outer = slabs_of(phases)
+    inner = phases // outer
+    slab, place = me // inner, lax.rem(me, inner)
     below = (lat + lats - 1) // lats
     above = (2 * lats - 2 - lat) // lats
     span = window.shape[2]
@@ -69,12 +89,10 @@
 
     barrier = pltpu.get_barrier_semaphore()
 
-    def greet(step, carry):
-        peer = lax.rem(me + step, phases)
-        pl.semaphore_signal(barrier, inc=1, device_id={"phase": peer})
-        return carry
-
-    lax.fori_loop(1, phases, greet, 0)
+    for step in range(1, outer):
+        pl.semaphore_signal(barrier, inc=1, device_id={"phase": partner(slab, step, outer) * inner + place})
+    for step in range(1, inner):
+        pl.semaphore_signal(barrier, inc=1, device_id={"phase": slab * inner + partner(place, step, inner)})
 
     @pl.when(lat > 0)
     def _():
@@ -115,35 +133,84 @@
         waves[field] = zero
         pulled[field] = zero
 
-    pl.semaphore_wait(barrier, phases - 1 + below + above)
-
-    def gather_copy(which, step, sending):
-        peer = lax.rem(me + step, phases)
-        at = pl.ds(me * share, share)
+    pl.semaphore_wait(barrier, outer - 1 + inner - 1 + below + above)
+
+    def chunk(group, at):
+        return pl.ds((group * inner + at) * share, share)
+
+    def outer_gather(which, step):
+        at = chunk(slab, place)
         return pltpu.make_async_remote_copy(
             src_ref=gathered.at[which, :, at],
             dst_ref=gathered.at[which, :, at],
-            send_sem=gather_send.at[which, step],
-            recv_sem=gather_recv.at[which, step],
-            device_id={"phase": peer},
-        )
-
-    def sum_copy(which, step):
-        peer = lax.rem(me + step, phases)
+            send_sem=outer_send.at[which, step],
+            recv_sem=outer_recv.at[which, step],
+            device_id={"phase": partner(slab, step, outer) * inner + place},
+        )
+
+    def inner_gather(which, held, step):
+        at = chunk(source_of(slab, held, outer), place)
         return pltpu.make_async_remote_copy(
-            src_ref=partial.at[which, :, pl.ds(peer * share, share)],
-            dst_ref=parts.at[which, step],
-            send_sem=sum_send.at[which, step],
-            recv_sem=sum_recv.at[which, step],
-            device_id={"phase": peer},
-        )
-
-    def each_peer(fn):
-        def body(step, carry):
-            fn(step)
-            return carry
-
-        lax.fori_loop(1, phases, body, 0)
+            src_ref=gathered.at[which, :, at],
+            dst_ref=gathered.at[which, :, at],
+            send_sem=inner_send.at[which, held, step],
+            recv_sem=inner_recv.at[which, held, step],
+            device_id={"phase": slab * inner + partner(place, step, inner)},
+        )
+
+    def inner_sum(which, held, step):
+        peer = partner(place, step, inner)
+        return pltpu.make_async_remote_copy(
+            src_ref=partial.at[which, :, chunk(partner(slab, held, outer), peer)],
+            dst_ref=parts.at[which, held, step],
+            send_sem=inner_send.at[2 + which, held, step],
+            recv_sem=inner_recv.at[2 + which, held, step],
+            device_id={"phase": slab * inner + peer},
+        )
+
+    def outer_sum(which, step):
+        return pltpu.make_async_remote_copy(
+            src_ref=staged.at[which, step],
+            dst_ref=parts.at[which, step, 0],
+            send_sem=outer_send.at[2 + which, step],
+            recv_sem=outer_recv.at[2 + which, step],
+            device_id={"phase": partner(slab, step, outer) * inner + place},
+        )
+
+    def gather_start(which):
+        for step in range(1, outer):
+            outer_gather(which, step).start()
+        for step in range(1, inner):
+            inner_gather(which, 0, step).start()
+
+    def gather_finish(which):
+        for held in range(1, outer):
+            outer_gather(which, held).wait_recv()
+            for step in range(1, inner):
+                inner_gather(which, held, step).start()
+        for step in range(1, outer):
+            outer_gather(which, step).wait_send()
+        for held in range(outer):
+            for step in range(1, inner):
+                inner_gather(which, held, step).wait()
+
+    def sum_over_phase(which):
+        order = list(reversed(range(outer)))
+        for held in order:
+            for step in range(1, inner):
+                inner_sum(which, held, step).start()
+        for held in order:
+            total = partial[which, :, chunk(partner(slab, held, outer), place)]
+            for step in range(1, inner):
+                inner_sum(which, held, step).wait()
+                total = total + parts[which, held, step]
+            if held > 0:
+                staged[which, held] = total
+                outer_sum(which, held).start()
+        for step in range(1, outer):
+            outer_sum(which, step).wait()
+            total = total + parts[which, step, 0]
+        return total
 
     def edge_copies(array, index):
         up = pltpu.make_async_remote_copy(
@@ -256,10 +323,10 @@
         pulled[2, mid] = -(mid_east * lon_diff(north[1:-1]) + mid_north * (north[2:] - north[:-2]))
 
     edges_start(coef_field, 2)
-    each_peer(lambda step: gather_copy(0, step, True).start())
+    gather_start(0)
 
     for which in range(2):
-        each_peer(lambda step: gather_copy(which, step, False).wait())
+        gather_finish(which)
         tile = window.at[which]
         for field in range(3):
             tile[field, HALO : HALO + rows] = gathered[which, field]
@@ -278,15 +345,11 @@
         for_blocks(DEG, advect)
         exponential(pulled, 1, DEG, keep_partial, 0)
 
-        each_peer(lambda step: sum_copy(which, step).start())
-        total = partial[which, :, pl.ds(me * share, share)]
-        each_peer(lambda step: sum_copy(which, step).wait())
-        for step in range(1, phases):
-            total = total + parts[which, step]
+        total = sum_over_phase(which)
         if which == 0:
             first[...] = total
             gathered[1, :, pl.ds(me * share, share)] = own[...] + time_step * total
-            each_peer(lambda step: gather_copy(1, step, True).start())
+            gather_start(1)
         else:
             first[...] = 0.5 * (first[...] + total)
 
@@ -303,6 +366,8 @@
 def per_device(phases, lats, state_now, ocean_depth, coriolis, phase_times, phase_weights):
     rows, share = ocean_depth.shape[0], state_now.shape[1]
     span = rows + 2 * HALO
+    outer = slabs_of(phases)
+    inner = phases // outer
     tile = (SUBLANES, LANES)
     vmem = pl.BlockSpec(memory_space=pltpu.VMEM)
     smem = pl.BlockSpec(memory_space=pltpu.SMEM)
@@ -326,13 +391,14 @@
             scratch(3, span),
             scratch(3, span),
             scratch(2, 3, rows),
-            scratch(2, phases, 3, share),
+            scratch(2, outer, inner, 3, share),
+            scratch(2, outer, 3, share),
             scratch(3, share),
             scratch(2, DEG + 1),
-            pltpu.SemaphoreType.DMA((2, phases)),
-            pltpu.SemaphoreType.DMA((2, phases)),
-            pltpu.SemaphoreType.DMA((2, phases)),
-            pltpu.SemaphoreType.DMA((2, phases)),
+            pltpu.SemaphoreType.DMA((4, outer)),
+            pltpu.SemaphoreType.DMA((4, outer)),
+            pltpu.SemaphoreType.DMA((4, outer, inner)),
+            pltpu.SemaphoreType.DMA((4, outer, inner)),
             pltpu.SemaphoreType.DMA((3, 2)),
             pltpu.SemaphoreType.DMA((3, 2)),
         ],

time: 65.2 us -> 58.8 us (0.902); the launches traced: 64.2 us -> 58.6 us
  Pallas kernels: 60.3 us -> 54.7 us
    pallas_call x1, Pallas kernels: 60.3 us -> 54.7 us  [per_device(): pl.pallas_call(functools.partial(kernel, phases, lats), out_shape=(out, o...]
where the time goes in v2:
time: 58.8 us; the launch traced here: 58.6 us
  Pallas kernels  54.7 us (93%)
  local copies, waits for them, and re-layouts  1.96 us (3%)
  between operations  1.94 us (3%)
    pallas_call x1, Pallas kernels, per_device(): pl.pallas_call(functools.partial(kernel, phases, lats), out_shape=(out, o...  54.7 us
    unnamed x4, local copies, waits for them, and re-layouts  1.96 us

profile of v2, /device:TPU:0, one launch (start us, length us, event | category | flops | bytes accessed | tf_op | source)
XLA Modules:
  0.0 58.6 jit_solution(17074560659422521465)
XLA Ops:
  1.9 54.7 %shard_map.68 = (f32[3,2,1024]{2,1,0:T(2,128)}, f32[3,2,1024]{2,1,0:T(2,128)}) custom-call(f32[3,2,1024]{2,1,0:T(2,128)} %state.1, f32[32,1024]{1,0:T(8,128)} %depth.1, f32[32]{0:T(128)} %coriolis.1, f32[1]{0:T(128)S(6)} %copy.9.times, f32[1]{0:T(128)S(6)} %copy.10.weights), custom_call_target="tpu_custom_call" | custom-call | tf_op jit(solution)/shard_map/pallas_call | solution.py:379
  56.6 0.0 copy-start
  56.6 1.4 %copy.11 = f32[3,2,1024]{2,1,0:T(2,128)} copy(f32[3,2,1024]{2,1,0:T(2,128)} %get-tuple-element.4) | data formatting | bytes 49152
  58.0 0.0 copy-done
  58.0 0.6 %copy.12 = f32[3,2,1024]{2,1,0:T(2,128)} copy(f32[3,2,1024]{2,1,0:T(2,128)S(1)} %copy-done) | data formatting | bytes 49152
Async XLA Ops:
  56.6 1.4 %copy-start = (f32[3,2,1024]{2,1,0:T(2,128)S(1)}, f32[3,2,1024]{2,1,0:T(2,128)}, u32[]{:S(2)}) copy-start(f32[3,2,1024]{2,1,0:T(2,128)} %get-tuple-element.5) | copy-start | bytes 73732

commit v3 on v2

--- a/solution.py
+++ b/solution.py
@@ -42,13 +42,14 @@
 def kernel(
     phases,
     lats,
-    state,
-    depth,
+    state_in,
+    depth_in,
     coriolis,
     times,
     weights,
-    next_out,
     tend_out,
+    state,
+    depth,
     own,
     gathered,
     window,
@@ -68,6 +69,7 @@
     inner_recv,
     halo_send,
     halo_recv,
+    input_sem,
 ):
     rows, share = depth.shape[0], state.shape[1]
     me, lat = lax.axis_index("phase"), lax.axis_index("lat")
@@ -78,6 +80,19 @@
     above = (2 * lats - 2 - lat) // lats
     span = window.shape[2]
 
+    copies = [
+        pltpu.make_async_copy(state_in, state, input_sem.at[0]),
+        pltpu.make_async_copy(depth_in, depth, input_sem.at[1]),
+    ]
+    for copy in copies:
+        copy.start()
+    barrier = pltpu.get_barrier_semaphore()
+
+    for step in range(1, outer):
+        pl.semaphore_signal(barrier, inc=1, device_id={"phase": partner(slab, step, outer) * inner + place})
+    for step in range(1, inner):
+        pl.semaphore_signal(barrier, inc=1, device_id={"phase": slab * inner + partner(place, step, inner)})
+
     zero = jnp.zeros((HALO, SUBLANES, LANES), jnp.float32)
     for array in (window.at[0], window.at[1]):
         for field in range(3):
@@ -87,13 +102,6 @@
         coef_field[field, 0:HALO] = zero
         coef_field[field, HALO + rows : span] = zero
 
-    barrier = pltpu.get_barrier_semaphore()
-
-    for step in range(1, outer):
-        pl.semaphore_signal(barrier, inc=1, device_id={"phase": partner(slab, step, outer) * inner + place})
-    for step in range(1, inner):
-        pl.semaphore_signal(barrier, inc=1, device_id={"phase": slab * inner + partner(place, step, inner)})
-
     @pl.when(lat > 0)
     def _():
         pl.semaphore_signal(barrier, inc=1, device_id={"lat": lat - 1})
@@ -102,36 +110,12 @@
     def _():
         pl.semaphore_signal(barrier, inc=1, device_id={"lat": lat + 1})
 
+    copies[0].wait()
     for s in range(SUBLANES):
-        lanes = pl.ds(s * LANES, LANES)
         for field in range(3):
-            piece = state[field, :, lanes]
+            piece = state[field, :, s * LANES : (s + 1) * LANES]
             own[field, :, s, :] = piece * HEIGHT_SCALE if field == 0 else piece
-        coef_field[0, HALO : HALO + rows, s, :] = depth[:, lanes] * DEPTH_SCALE
-    for row in range(rows):
-        coef_field[1, HALO + row] = jnp.full((SUBLANES, LANES), coriolis[row] * ROTATION_SCALE, jnp.float32)
     gathered[0, :, pl.ds(me * share, share)] = own[...]
-
-    half_time = jnp.full((SUBLANES, LANES), times[0] * 0.5, jnp.float32)
-    weight = jnp.full((SUBLANES, LANES), weights[0], jnp.float32)
-    square = half_time * half_time
-    power = jnp.ones_like(half_time)
-    for degree in range(DEG + 1):
-        summed = jnp.zeros_like(square)
-        for term in reversed(range(series_terms)):
-            factor = (-1.0) ** term / (math.factorial(term) * math.factorial(term + degree))
-            summed = summed * square + factor
-        value = summed * power
-        if degree > 0:
-            value = 2.0 * value
-        series[0, degree] = value
-        series[1, degree] = weight * (value if degree % 2 == 0 else -value)
-        power = power * half_time
-
-    zero = jnp.zeros((span, SUBLANES, LANES), jnp.float32)
-    for field in range(3):
-        waves[field] = zero
-        pulled[field] = zero
 
     pl.semaphore_wait(barrier, outer - 1 + inner - 1 + below + above)
 
@@ -290,12 +274,14 @@
 
         for_blocks(margin, body)
 
-    def exponential(base, direction, margin, store, last_margin):
+    def fill(base, direction, start, count):
+        at = pl.ds(start, count)
         top = series[direction, DEG]
         for field in range(3):
-            even[field] = top * base[field]
-            odd[field] = jnp.zeros((span, SUBLANES, LANES), jnp.float32)
-
+            even[field, at] = top * base[field, at]
+            odd[field, at] = jnp.zeros((count, SUBLANES, LANES), jnp.float32)
+
+    def exponential(base, direction, margin, store, last_margin):
         def two_steps(j, carry):
             clenshaw(odd, even, base, series[direction, DEG - 1 - 2 * j], margin)
             clenshaw(even, odd, base, series[direction, DEG - 2 - 2 * j], margin)
@@ -322,8 +308,36 @@
         pulled[1, mid] = -(mid_east * lon_diff(east[1:-1]) + mid_north * (east[2:] - east[:-2]))
         pulled[2, mid] = -(mid_east * lon_diff(north[1:-1]) + mid_north * (north[2:] - north[:-2]))
 
+    gather_start(0)
+
+    copies[1].wait()
+    for s in range(SUBLANES):
+        coef_field[0, HALO : HALO + rows, s, :] = depth[:, s * LANES : (s + 1) * LANES] * DEPTH_SCALE
+    for row in range(rows):
+        coef_field[1, HALO + row] = jnp.full((SUBLANES, LANES), coriolis[row] * ROTATION_SCALE, jnp.float32)
     edges_start(coef_field, 2)
-    gather_start(0)
+
+    half_time = jnp.full((SUBLANES, LANES), times[0] * 0.5, jnp.float32)
+    weight = jnp.full((SUBLANES, LANES), weights[0], jnp.float32)
+    square = half_time * half_time
+    power = jnp.ones_like(half_time)
+    for degree in range(DEG + 1):
+        summed = jnp.zeros_like(square)
+        for term in reversed(range(series_terms)):
+            factor = (-1.0) ** term / (math.factorial(term) * math.factorial(term + degree))
+            summed = summed * square + factor
+        value = summed * power
+        if degree > 0:
+            value = 2.0 * value
+        series[0, degree] = value
+        series[1, degree] = weight * (value if degree % 2 == 0 else -value)
+        power = power * half_time
+
+    zero = jnp.zeros((span, SUBLANES, LANES), jnp.float32)
+    for field in range(3):
+        waves[field] = zero
+        pulled[field] = zero
+
 
     for which in range(2):
         gather_finish(which)
@@ -331,9 +345,12 @@
         for field in range(3):
             tile[field, HALO : HALO + rows] = gathered[which, field]
         edges_start(tile, which)
+        fill(tile, 0, HALO, rows)
         if which == 0:
             edges_wait(coef_field, 2)
         edges_wait(tile, which)
+        fill(tile, 0, 0, HALO)
+        fill(tile, 0, HALO + rows, HALO)
 
         def keep_wave(field, at, value):
             waves[field, pl.ds(at, BLOCK)] = value
@@ -343,6 +360,7 @@
 
         exponential(tile, 0, 2 * DEG, keep_wave, 2 * DEG)
         for_blocks(DEG, advect)
+        fill(pulled, 1, 0, span)
         exponential(pulled, 1, DEG, keep_partial, 0)
 
         total = sum_over_phase(which)
@@ -360,7 +378,11 @@
             if field == 0:
                 piece = piece * radius_scale
             tend_out[field, :, lanes] = piece
-            next_out[field, :, lanes] = state[field, :, lanes] + time_step * piece
+
+
+def finish(state, tendency, next_out, tend_out):
+    tend_out[...] = tendency[...]
+    next_out[...] = state[...] + time_step * tendency[...]
 
 
 def per_device(phases, lats, state_now, ocean_depth, coriolis, phase_times, phase_weights):
@@ -376,12 +398,15 @@
     def scratch(*shape):
         return pltpu.VMEM(shape + tile, jnp.float32)
 
-    return pl.pallas_call(
+    any_space = pl.BlockSpec(memory_space=pl.ANY)
+    tendency = pl.pallas_call(
         functools.partial(kernel, phases, lats),
-        out_shape=(out, out),
-        in_specs=[vmem, vmem, smem, smem, smem],
-        out_specs=(vmem, vmem),
+        out_shape=out,
+        in_specs=[any_space, any_space, smem, smem, smem],
+        out_specs=vmem,
         scratch_shapes=[
+            pltpu.VMEM(state_now.shape, jnp.float32),
+            pltpu.VMEM(ocean_depth.shape, jnp.float32),
             scratch(3, share),
             scratch(2, 3, rows),
             scratch(2, 3, span),
@@ -401,9 +426,16 @@
             pltpu.SemaphoreType.DMA((4, outer, inner)),
             pltpu.SemaphoreType.DMA((3, 2)),
             pltpu.SemaphoreType.DMA((3, 2)),
+            pltpu.SemaphoreType.DMA((2,)),
         ],
         compiler_params=pltpu.CompilerParams(collective_id=0, has_side_effects=True),
     )(state_now, ocean_depth, coriolis, phase_times, phase_weights)
+    return pl.pallas_call(
+        finish,
+        out_shape=(out, out),
+        in_specs=[vmem, vmem],
+        out_specs=(vmem, vmem),
+    )(state_now, tendency)
 
 
 def solution(mesh):

time: 58.8 us -> 57.8 us (0.983)
  local copies, waits for them, and re-layouts: 1.96 us -> 0 us
  Pallas kernels: 54.7 us -> 55.6 us
    unnamed x4 -> x0, local copies, waits for them, and re-layouts: 1.96 us -> none
    pallas_call x1 -> x2, Pallas kernels: 54.7 us -> 55.6 us  [the longest x1 54.2 us: per_device(): pl.pallas_call(functools.partial(kernel, phases, lats), out_shape=out, in...]
where the time goes in v3:
time: 57.8 us; the launch traced here: 57.5 us
  Pallas kernels  55.6 us (96%)
  between operations  1.93 us (3%)
    pallas_call x1, Pallas kernels, per_device(): pl.pallas_call(functools.partial(kernel, phases, lats), out_shape=out, in...  54.2 us
    pallas_call x1, Pallas kernels, per_device(): pl.pallas_call(finish, out_shape=(out, out), in_specs=[vmem, vmem], out_s...  1.38 us

profile of v3, /device:TPU:0, one launch (start us, length us, event | category | flops | bytes accessed | tf_op | source)
XLA Modules:
  0.0 57.5 jit_solution(16473788458218320985)
XLA Ops:
  1.9 54.2 %shard_map.68.tendency = f32[3,2,1024]{2,1,0:T(2,128)} custom-call(f32[3,2,1024]{2,1,0:T(2,128)} %state.1, f32[32,1024]{1,0:T(8,128)} %depth_in.1, f32[32]{0:T(128)} %coriolis.1, f32[1]{0:T(128)S(6)} %copy.7.times, f32[1]{0:T(128)S(6)} %copy.8.weights), custom_call_target="tpu_custom_call" | custom-call | tf_op jit(solution)/shard_map/pallas_call | solution.py:402
  56.2 1.4 %shard_map.69 = (f32[3,2,1024]{2,1,0:T(2,128)}, f32[3,2,1024]{2,1,0:T(2,128)}) custom-call(f32[3,2,1024]{2,1,0:T(2,128)} %state.1, f32[3,2,1024]{2,1,0:T(2,128)} %shard_map.68.tendency), custom_call_target="tpu_custom_call" | custom-call | tf_op jit(solution)/shard_map/pallas_call | solution.py:433
